TPU v7x, 256 devices: a whole 4x4x8 slice. The times are simulated.
256 devices in a mesh: word: 16 (over z_lo, x, core), ctx: 16 (over y, z_hi).
Axes of the slice: x: 4, y: 4, z: 8 (z_hi: 4, z_lo: 2; z = z_hi * 2 + z_lo), core: 2. Of those that a mesh axis runs over, the one named last changes fastest.
Arguments:
- counts: int32 [24576, 24576], P('word', 'ctx'), may hold values from 0 to 1800, as said below
- word_vecs: float32 [24576, 300], P(('word', 'ctx')), may hold values from -0.35 to 0.35
- word_bias: float32 [24576], P(('word', 'ctx')), may hold values from 0.5 to 3
- word_accum: float32 [24576, 300], P(('word', 'ctx')), may hold values from 1.6276042e-06 to 8.138021e-05
- word_bias_accum: float32 [24576], P(('word', 'ctx')), may hold values from 1 to 30
- ctx_vecs: float32 [24576, 300], P(('ctx', 'word')), may hold values from -0.35 to 0.35
- ctx_bias: float32 [24576], P(('ctx', 'word')), may hold values from 0.5 to 3
- ctx_accum: float32 [24576, 300], P(('ctx', 'word')), may hold values from 1.6276042e-06 to 8.138021e-05
- ctx_bias_accum: float32 [24576], P(('ctx', 'word')), may hold values from 1 to 30
Outputs:
- new_word_vecs: float32 [24576, 300], P(('word', 'ctx'))
- new_word_bias: float32 [24576], P(('word', 'ctx'))
- new_word_accum: float32 [24576, 300], P(('word', 'ctx'))
- new_word_bias_accum: float32 [24576], P(('word', 'ctx'))
- new_ctx_vecs: float32 [24576, 300], P(('ctx', 'word'))
- new_ctx_bias: float32 [24576], P(('ctx', 'word'))
- new_ctx_accum: float32 [24576, 300], P(('ctx', 'word'))
- new_ctx_bias_accum: float32 [24576], P(('ctx', 'word'))
Inputs may be any that keep to these rules, and one draw needn't show every extreme that they name: counts are non-negative integers, and a count is zero exactly where the word and the context never co-occur.
All inputs are finite; a program needn't handle non-finite values.
Results may differ from a plain program's by a relative error of at most 0.0045.
Values may be sent and summed in bfloat16 or wider, within the bound.
No kernel may reach another device: no remote copies, remote signals or barrier semaphores. Data moves between devices by JAX's collectives and lax.ppermute only.
A program may use at most 64 MiB of HBM per device.

v0:
```python
import jax
import jax.numpy as jnp
from jax import lax
from jax.sharding import PartitionSpec as P

count_cap = 100.0
power_law = 0.75
step_rate = 0.2


def weighted_residual(tile_counts, word_rows, ctx_rows, word_bias_rows, ctx_bias_rows):
    values = tile_counts.astype(jnp.float32)
    log_count = jnp.log(jnp.maximum(values, 1.0))
    weight = jnp.where(tile_counts > 0, jnp.minimum((values / count_cap) ** power_law, 1.0), 0.0)
    inner = lax.dot_general(
        word_rows, ctx_rows, (((1,), (1,)), ((), ())), preferred_element_type=jnp.float32
    )
    return weight * (inner + word_bias_rows[:, None] + ctx_bias_rows[None, :] - log_count)


def adagrad(param, accum, grad):
    new_accum = accum + grad * grad
    return (param - step_rate * grad / jnp.sqrt(new_accum), new_accum)


def per_device(
    counts,
    word_vecs,
    word_bias,
    word_accum,
    word_bias_accum,
    ctx_vecs,
    ctx_bias,
    ctx_accum,
    ctx_bias_accum,
):
    word_rows, word_bias_rows = (
        lax.all_gather(word_vecs.astype(jnp.bfloat16), "ctx", axis=0, tiled=True),
        lax.all_gather(word_bias.astype(jnp.bfloat16), "ctx", axis=0, tiled=True),
    )
    ctx_rows, ctx_bias_rows = (
        lax.all_gather(ctx_vecs.astype(jnp.bfloat16), "word", axis=0, tiled=True),
        lax.all_gather(ctx_bias.astype(jnp.bfloat16), "word", axis=0, tiled=True),
    )
    scaled = weighted_residual(
        counts,
        word_rows,
        ctx_rows,
        word_bias_rows.astype(jnp.float32),
        ctx_bias_rows.astype(jnp.float32),
    )
    scaled_low = scaled.astype(jnp.bfloat16)
    word_term = jnp.dot(scaled_low, ctx_rows, preferred_element_type=jnp.float32)
    word_bias_term = jnp.sum(scaled, axis=1)
    ctx_term = lax.dot_general(
        scaled_low, word_rows, (((0,), (0,)), ((), ())), preferred_element_type=jnp.float32
    )
    ctx_bias_term = jnp.sum(scaled, axis=0)
    word_owned = word_vecs.shape[0]
    ctx_owned = ctx_vecs.shape[0]
    word_total, word_bias_total = lax.psum((word_term, word_bias_term), "ctx")
    ctx_total, ctx_bias_total = lax.psum((ctx_term, ctx_bias_term), "word")
    word_start = lax.axis_index("ctx") * word_owned
    ctx_start = lax.axis_index("word") * ctx_owned
    word_sum = lax.dynamic_slice_in_dim(word_total, word_start, word_owned, 0)
    word_bias_sum = lax.dynamic_slice_in_dim(word_bias_total, word_start, word_owned, 0)
    ctx_sum = lax.dynamic_slice_in_dim(ctx_total, ctx_start, ctx_owned, 0)
    ctx_bias_sum = lax.dynamic_slice_in_dim(ctx_bias_total, ctx_start, ctx_owned, 0)
    all_contexts = counts.shape[1] * lax.axis_size("ctx")
    all_words = counts.shape[0] * lax.axis_size("word")
    word_scale = 2.0 / all_contexts
    ctx_scale = 2.0 / all_words
    new_word_vecs, new_word_accum = adagrad(word_vecs, word_accum, word_scale * word_sum)
    new_word_bias, new_word_bias_accum = adagrad(
        word_bias, word_bias_accum, word_scale * word_bias_sum
    )
    new_ctx_vecs, new_ctx_accum = adagrad(ctx_vecs, ctx_accum, ctx_scale * ctx_sum)
    new_ctx_bias, new_ctx_bias_accum = adagrad(ctx_bias, ctx_bias_accum, ctx_scale * ctx_bias_sum)
    return (
        new_word_vecs,
        new_word_bias,
        new_word_accum,
        new_word_bias_accum,
        new_ctx_vecs,
        new_ctx_bias,
        new_ctx_accum,
        new_ctx_bias_accum,
    )


def solution(mesh):
    return jax.shard_map(
        per_device,
        mesh=mesh,
        in_specs=(
            P("word", "ctx"),
            P(("word", "ctx"), None),
            P(("word", "ctx")),
            P(("word", "ctx"), None),
            P(("word", "ctx")),
            P(("ctx", "word"), None),
            P(("ctx", "word")),
            P(("ctx", "word"), None),
            P(("ctx", "word")),
        ),
        out_specs=(
            P(("word", "ctx"), None),
            P(("word", "ctx")),
            P(("word", "ctx"), None),
            P(("word", "ctx")),
            P(("ctx", "word"), None),
            P(("ctx", "word")),
            P(("ctx", "word"), None),
            P(("ctx", "word")),
        ),
        check_vma=False,
    )
```

profile of v0, /device:TPU:1, one launch (start us, length us, event | category | flops | bytes accessed | tf_op | source)
XLA Modules:
  0.0 501.2 jit_solution(13768359193963411753)
XLA Ops:
  7.2 1.3 dynamic-slice.1
  8.5 1.3 dynamic-slice
  11.0 0.7 convert_element_type.27
  11.7 0.7 convert_element_type.29
  12.4 0.2 dynamic-update-slice.1
  12.6 29.7 %all-reduce.1 = bf16[1536]{0:T(1024)(128)(2,1)S(1)} all-reduce(bf16[1536]{0:T(1024)(128)(2,1)S(1)} %dynamic-update-slice.1), channel_id=1, replica_groups=mesh['word'=16,'ctx'=16] {'word'}, use_global_device_ids=true, to_apply=%add.1 | all-reduce | flops 1536 | bytes 6144
  42.3 0.2 dynamic-update-slice
  42.5 39.1 %all-reduce = bf16[1536]{0:T(1024)(128)(2,1)S(1)} all-reduce(bf16[1536]{0:T(1024)(128)(2,1)S(1)} %dynamic-update-slice), channel_id=1, replica_groups=mesh['word'=16,'ctx'=16] {'ctx'}, use_global_device_ids=true, to_apply=%add | all-reduce | flops 1536 | bytes 6144
  81.7 0.9 convert_element_type.25
  82.6 0.9 convert_element_type.26
  83.5 30.2 %all_gather.13 = bf16[1536,300]{1,0:T(8,128)(2,1)S(1)} all-gather(bf16[96,300]{1,0:T(8,128)(2,1)S(1)} %convert_element_type.26), channel_id=1, replica_groups=mesh['word'=16,'ctx'=16] {'word'}, dimensions={0}, use_global_device_ids=true | all-gather | bytes 979200 | tf_op jit(solution)/shard_map/all_gather | solution.py:42
  113.7 46.0 %all_gather.12 = bf16[1536,300]{1,0:T(8,128)(2,1)S(1)} all-gather(bf16[96,300]{1,0:T(8,128)(2,1)S(1)} %convert_element_type.25), channel_id=1, replica_groups=mesh['word'=16,'ctx'=16] {'ctx'}, dimensions={0}, use_global_device_ids=true | all-gather | bytes 979200 | tf_op jit(solution)/shard_map/all_gather | solution.py:38
  159.7 15.2 %fusion.4 = (f32[1536]{0:T(1024)S(1)}, f32[1536]{0:T(1024)S(1)}, bf16[1536,1536]{1,0:T(8,128)(2,1)S(1)}) fusion(f32[1536]{0:T(1024)S(1)} %convert_element_type.30, f32[1536]{0:T(1024)S(1)} %convert_element_type.28, bf16[1536,300]{1,0:T(8,128)(2,1)S(1)} %all_gather.12, bf16[1536,300]{1,0:T(8,128)(2,1)S(1)} %all_gather.13, s32[1536,1536]{1,0:T(8,128)} %param.9), kind=kOutput, calls=%fused_computation.14 | convolution fusion | flops 1446245376 | bytes 16023552 | tf_op jit(solution)/shard_map/dot_general | solution.py:15
  175.0 2.1 copy-done.8
  177.1 4.1 fusion.2
  181.4 6.5 %fusion = f32[1536,300]{1,0:T(8,128)} fusion(bf16[1536,300]{1,0:T(8,128)(2,1)S(1)} %all_gather.12, bf16[1536,1536]{1,0:T(8,128)(2,1)} %copy-done.8), kind=kOutput, calls=%fused_computation.2 | convolution fusion | flops 1415577600 | bytes 7483392 | tf_op jit(solution)/shard_map/dot_general | solution.py:55
  187.9 33.8 %psum.31 = f32[1536]{0:T(1024)S(1)} all-reduce(f32[1536]{0:T(1024)S(1)} %get-tuple-element.8), channel_id=1, replica_groups=mesh['word'=16,'ctx'=16] {'word'}, use_global_device_ids=true, to_apply=%region_5.6 | all-reduce | flops 1536 | bytes 12288 | tf_op jit(solution)/shard_map/psum | solution.py:62
  221.7 35.5 %psum.29 = f32[1536]{0:T(1024)S(1)} all-reduce(f32[1536]{0:T(1024)S(1)} %get-tuple-element.9), channel_id=1, replica_groups=mesh['word'=16,'ctx'=16] {'ctx'}, use_global_device_ids=true, to_apply=%region_2.3 | all-reduce | flops 1536 | bytes 12288 | tf_op jit(solution)/shard_map/psum | solution.py:61
  257.2 0.6 multiply_subtract_fusion.2
  257.8 0.6 multiply_subtract_fusion.3
  258.4 95.9 %all-reduce.5.cloned.1.call-done = f32[1536,300]{1,0:T(8,128)} async-done(((f32[1536,300]{1,0:T(8,128)}), f32[1536,300]{1,0:T(8,128)}) %all-reduce.5.cloned.1.call-update) | async-done | bytes 1843216 | tf_op jit(solution)/shard_map/psum | solution.py:61
  354.3 1.7 multiply_subtract_fusion.1
  356.0 136.8 %all-reduce.7.cloned.1.call-done = f32[1536,300]{1,0:T(8,128)} async-done(((f32[1536,300]{1,0:T(8,128)}), f32[1536,300]{1,0:T(8,128)}) %all-reduce.7.cloned.1.call-update) | async-done | bytes 1843216 | tf_op jit(solution)/shard_map/psum | solution.py:62
  492.7 1.7 multiply_subtract_fusion
  (25 shorter events, 0.2 us)
Async XLA Ops:
  7.2 347.1 %all-reduce.5.cloned.1.call-start = ((), (), s32[]{:S(2)}) async-start(), calls=%async_computation | async-start | bytes 4718592 | tf_op jit(solution)/shard_map/psum | solution.py:61
  174.9 2.1 copy-start.8
  181.2 76.0 %copy-start.4 = (f32[96]{0:T(128)S(1)}, f32[96]{0:T(128)}, u32[]{:S(2)}) copy-start(f32[96]{0:T(128)} %param.15) | copy-start | bytes 1156
  181.2 76.0 %copy-start.5 = (f32[96]{0:T(128)S(1)}, f32[96]{0:T(128)}, u32[]{:S(2)}) copy-start(f32[96]{0:T(128)} %param.17) | copy-start | bytes 1156
  181.2 76.6 %copy-start.6 = (f32[96]{0:T(128)S(1)}, f32[96]{0:T(128)}, u32[]{:S(2)}) copy-start(f32[96]{0:T(128)} %param.11) | copy-start | bytes 1156
  181.2 76.6 %copy-start.7 = (f32[96]{0:T(128)S(1)}, f32[96]{0:T(128)}, u32[]{:S(2)}) copy-start(f32[96]{0:T(128)} %param.13) | copy-start | bytes 1156
  181.3 173.1 %copy-start = (f32[96,300]{1,0:T(8,128)S(1)}, f32[96,300]{1,0:T(8,128)}, u32[]{:S(2)}) copy-start(f32[96,300]{1,0:T(8,128)} %param.10) | copy-start | bytes 345604
  181.3 173.0 %copy-start.2 = (f32[96,300]{1,0:T(8,128)S(1)}, f32[96,300]{1,0:T(8,128)}, u32[]{:S(2)}) copy-start(f32[96,300]{1,0:T(8,128)} %param.12) | copy-start | bytes 345604
  181.3 311.5 %copy-start.1 = (f32[96,300]{1,0:T(8,128)S(1)}, f32[96,300]{1,0:T(8,128)}, u32[]{:S(2)}) copy-start(f32[96,300]{1,0:T(8,128)} %param.14) | copy-start | bytes 345604
  181.3 311.4 %copy-start.3 = (f32[96,300]{1,0:T(8,128)S(1)}, f32[96,300]{1,0:T(8,128)}, u32[]{:S(2)}) copy-start(f32[96,300]{1,0:T(8,128)} %param.16) | copy-start | bytes 345604
  181.3 311.4 %all-reduce.7.cloned.1.call-start = ((), (), s32[]{:S(2)}) async-start(), calls=%async_computation.1 | async-start | bytes 4718592 | tf_op jit(solution)/shard_map/psum | solution.py:62
Sparse Core Ops, SparseCore 0:
  181.3 172.9 all-reduce.4
  357.0 135.7 all-reduce.6
where the time goes:
time: 502 us; the launch traced here: 501 us
  waiting for transfers between devices  233 us (46%)
  blocking collectives  214 us (43%)
  matrix products  25.9 us (5%)
  between operations  15.5 us (3%)
  other arithmetic  7.68 us (2%)
  local copies, waits for them, and re-layouts  5.14 us (1%)
    psum x1, waiting for transfers between devices, per_device(): ctx_total, ctx_bias_total = lax.psum((ctx_term, ctx_bias_term), 'word')  137 us
    psum x1, waiting for transfers between devices, per_device(): word_total, word_bias_total = lax.psum((word_term, word_bias_term), 'ctx')  95.9 us
    unnamed x2, blocking collectives  68.9 us
    all_gather x1, blocking collectives, per_device(): lax.all_gather(word_vecs.astype(jnp.bfloat16), 'ctx', axis=0, tiled=True)  46 us
    psum x1, blocking collectives, per_device(): word_total, word_bias_total = lax.psum((word_term, word_bias_term), 'ctx')  35.5 us
    psum x1, blocking collectives, per_device(): ctx_total, ctx_bias_total = lax.psum((ctx_term, ctx_bias_term), 'word')  33.8 us
    all_gather x1, blocking collectives, per_device(): lax.all_gather(ctx_vecs.astype(jnp.bfloat16), 'word', axis=0, tiled=True)  30.2 us
    dot_general x1, matrix products, weighted_residual(): lax.dot_general(word_rows, ctx_rows, (((1,), (1,)), ((), ())), preferred_...  15.2 us
  transfers between devices with their start and end apart: 2, of which 2 were waited for; matrix products, arithmetic and copies ran while one was open for 2% of the time, Pallas kernels for 0%

commit v1 on v0

--- a/solution.py
+++ b/solution.py
@@ -35,7 +35,12 @@
     ctx_bias_accum,
 ):
     word_rows, word_bias_rows = (
-        lax.all_gather(word_vecs.astype(jnp.bfloat16), "ctx", axis=0, tiled=True),
+        jnp.concatenate(
+            lax.all_to_all(
+                jnp.stack([word_vecs.astype(jnp.bfloat16)] * lax.axis_size("ctx")), "ctx", 0, 0
+            ),
+            axis=0,
+        ),
         lax.all_gather(word_bias.astype(jnp.bfloat16), "ctx", axis=0, tiled=True),
     )
     ctx_rows, ctx_bias_rows = (

time: 502 us -> 475 us (0.946)
  blocking collectives: 214 us -> 173 us
  starting transfers between devices: 0.08 us -> 11.8 us
    all_gather x1 -> x0, blocking collectives: 46 us -> none  [per_device(): lax.all_gather(word_vecs.astype(jnp.bfloat16), 'ctx', axis=0, tiled=True)]
    unnamed x2, blocking collectives: 68.9 us -> 82.2 us
    all_to_all x0 -> x1, starting transfers between devices: none -> 11.7 us  [per_device(): lax.all_to_all(jnp.stack([word_vecs.astype(jnp.bfloat16)] * lax.axis_size...]
  transfers between devices with their start and end apart: 2 -> 3, of which waited for: 2 -> 2; matrix products, arithmetic and copies ran while one was open for 2% -> 3% of each run, Pallas kernels for 0% -> 0%
where the time goes in v1:
time: 475 us
  waiting for transfers between devices  234 us (49%)
  blocking collectives  173 us (36%)
  matrix products  25.9 us (5%)
  between operations  15.5 us (3%)
  starting transfers between devices  11.8 us (2%)
  other arithmetic  7.68 us (2%)
  local copies, waits for them, and re-layouts  6.25 us (1%)
    psum x1, waiting for transfers between devices, per_device(): ctx_total, ctx_bias_total = lax.psum((ctx_term, ctx_bias_term), 'word')  137 us
    psum x1, waiting for transfers between devices, per_device(): word_total, word_bias_total = lax.psum((word_term, word_bias_term), 'ctx')  97.3 us
    unnamed x2, blocking collectives  82.2 us
    psum x1, blocking collectives, per_device(): word_total, word_bias_total = lax.psum((word_term, word_bias_term), 'ctx')  34.6 us
    psum x1, blocking collectives, per_device(): ctx_total, ctx_bias_total = lax.psum((ctx_term, ctx_bias_term), 'word')  29.1 us
    all_gather x1, blocking collectives, per_device(): lax.all_gather(ctx_vecs.astype(jnp.bfloat16), 'word', axis=0, tiled=True)  27.3 us
    dot_general x1, matrix products, weighted_residual(): lax.dot_general(word_rows, ctx_rows, (((1,), (1,)), ((), ())), preferred_...  15.2 us
    all_to_all x1, starting transfers between devices, per_device(): lax.all_to_all(jnp.stack([word_vecs.astype(jnp.bfloat16)] * lax.axis_size...  11.7 us
  transfers between devices with their start and end apart: 3, of which 2 were waited for; matrix products, arithmetic and copies ran while one was open for 3% of the time, Pallas kernels for 0%

profile of v1, /device:TPU:1, one launch (start us, length us, event | category | flops | bytes accessed | tf_op | source)
XLA Modules:
  0.0 474.5 jit_solution(9378802639082584400)
XLA Ops:
  7.2 0.9 convert_element_type.25
  8.1 1.1 stack.2
  9.2 11.7 %all-to-all-start = ((bf16[16,96,300]{2,1,0:T(8,128)(2,1)}), bf16[16,96,300]{2,1,0:T(8,128)(2,1)S(1)}, u32[]{:S(2)}, u32[]{:S(2)}) async-start(bf16[16,96,300]{2,1,0:T(8,128)(2,1)} %stack.2), calls=%async_computation | async-start | bytes 2359296 | tf_op jit(solution)/shard_map/all_to_all | solution.py:39
  21.0 1.3 dynamic-slice.1
  22.3 1.3 dynamic-slice
  24.8 0.7 convert_element_type.27
  25.5 0.7 convert_element_type.29
  26.3 40.2 %all-reduce.1 = bf16[1536]{0:T(1024)(128)(2,1)S(1)} all-reduce(bf16[1536]{0:T(1024)(128)(2,1)S(1)} %dynamic-update-slice.1), channel_id=1, replica_groups=mesh['word'=16,'ctx'=16] {'word'}, use_global_device_ids=true, to_apply=%add.1 | all-reduce | flops 1536 | bytes 6144
  66.6 0.2 dynamic-update-slice
  66.9 42.0 %all-reduce = bf16[1536]{0:T(1024)(128)(2,1)S(1)} all-reduce(bf16[1536]{0:T(1024)(128)(2,1)S(1)} %dynamic-update-slice), channel_id=1, replica_groups=mesh['word'=16,'ctx'=16] {'ctx'}, use_global_device_ids=true, to_apply=%add | all-reduce | flops 1536 | bytes 6144
  108.8 0.9 convert_element_type.26
  109.8 27.3 %all_gather.9 = bf16[1536,300]{1,0:T(8,128)(2,1)S(1)} all-gather(bf16[96,300]{1,0:T(8,128)(2,1)S(1)} %convert_element_type.26), channel_id=1, replica_groups=mesh['word'=16,'ctx'=16] {'word'}, dimensions={0}, use_global_device_ids=true | all-gather | bytes 979200 | tf_op jit(solution)/shard_map/all_gather | solution.py:47
  137.1 15.2 %fusion.4 = (f32[1536]{0:T(1024)S(1)}, f32[1536]{0:T(1024)S(1)}, bf16[1536,1536]{1,0:T(8,128)(2,1)S(1)}) fusion(f32[1536]{0:T(1024)S(1)} %convert_element_type.30, f32[1536]{0:T(1024)S(1)} %convert_element_type.28, bf16[1536,300]{1,0:T(8,128)(2,1)S(1)} %bitcast.9, bf16[1536,300]{1,0:T(8,128)(2,1)S(1)} %all_gather.9, s32[1536,1536]{1,0:T(8,128)} %param.9), kind=kOutput, calls=%fused_computation.14 | convolution fusion | flops 1446245376 | bytes 16023552 | tf_op jit(solution)/shard_map/dot_general | solution.py:15
  152.4 2.1 copy-done.8
  154.5 4.1 fusion.2
  158.8 6.5 %fusion = f32[1536,300]{1,0:T(8,128)} fusion(bf16[1536,300]{1,0:T(8,128)(2,1)S(1)} %bitcast.10, bf16[1536,1536]{1,0:T(8,128)(2,1)} %copy-done.8), kind=kOutput, calls=%fused_computation.2 | convolution fusion | flops 1415577600 | bytes 7483392 | tf_op jit(solution)/shard_map/dot_general | solution.py:60
  165.4 29.1 %psum.31 = f32[1536]{0:T(1024)S(1)} all-reduce(f32[1536]{0:T(1024)S(1)} %get-tuple-element.8), channel_id=1, replica_groups=mesh['word'=16,'ctx'=16] {'word'}, use_global_device_ids=true, to_apply=%region_5.6 | all-reduce | flops 1536 | bytes 12288 | tf_op jit(solution)/shard_map/psum | solution.py:67
  194.4 34.6 %psum.29 = f32[1536]{0:T(1024)S(1)} all-reduce(f32[1536]{0:T(1024)S(1)} %get-tuple-element.9), channel_id=1, replica_groups=mesh['word'=16,'ctx'=16] {'ctx'}, use_global_device_ids=true, to_apply=%region_2.3 | all-reduce | flops 1536 | bytes 12288 | tf_op jit(solution)/shard_map/psum | solution.py:66
  229.1 0.6 multiply_subtract_fusion.2
  229.7 0.6 multiply_subtract_fusion.3
  230.3 97.3 %all-reduce.5.cloned.1.call-done = f32[1536,300]{1,0:T(8,128)} async-done(((f32[1536,300]{1,0:T(8,128)}), f32[1536,300]{1,0:T(8,128)}) %all-reduce.5.cloned.1.call-update) | async-done | bytes 1843216 | tf_op jit(solution)/shard_map/psum | solution.py:66
  327.6 1.7 multiply_subtract_fusion.1
  329.3 136.8 %all-reduce.7.cloned.1.call-done = f32[1536,300]{1,0:T(8,128)} async-done(((f32[1536,300]{1,0:T(8,128)}), f32[1536,300]{1,0:T(8,128)}) %all-reduce.7.cloned.1.call-update) | async-done | bytes 1843216 | tf_op jit(solution)/shard_map/psum | solution.py:67
  466.0 1.7 multiply_subtract_fusion
  (27 shorter events, 0.4 us)
Async XLA Ops:
  9.2 127.9 %all-to-all-start = ((bf16[16,96,300]{2,1,0:T(8,128)(2,1)}), bf16[16,96,300]{2,1,0:T(8,128)(2,1)S(1)}, u32[]{:S(2)}, u32[]{:S(2)}) async-start(bf16[16,96,300]{2,1,0:T(8,128)(2,1)} %stack.2), calls=%async_computation | async-start | bytes 2359296 | tf_op jit(solution)/shard_map/all_to_all | solution.py:39
  20.9 306.7 %all-reduce.5.cloned.1.call-start = ((), (), s32[]{:S(2)}) async-start(), calls=%async_computation.1 | async-start | bytes 4718592 | tf_op jit(solution)/shard_map/psum | solution.py:66
  152.4 2.1 copy-start.8
  158.6 70.4 %copy-start.4 = (f32[96]{0:T(128)S(1)}, f32[96]{0:T(128)}, u32[]{:S(2)}) copy-start(f32[96]{0:T(128)} %param.15) | copy-start | bytes 1156
  158.7 70.4 %copy-start.5 = (f32[96]{0:T(128)S(1)}, f32[96]{0:T(128)}, u32[]{:S(2)}) copy-start(f32[96]{0:T(128)} %param.17) | copy-start | bytes 1156
  158.7 71.0 %copy-start.6 = (f32[96]{0:T(128)S(1)}, f32[96]{0:T(128)}, u32[]{:S(2)}) copy-start(f32[96]{0:T(128)} %param.11) | copy-start | bytes 1156
  158.7 71.0 %copy-start.7 = (f32[96]{0:T(128)S(1)}, f32[96]{0:T(128)}, u32[]{:S(2)}) copy-start(f32[96]{0:T(128)} %param.13) | copy-start | bytes 1156
  158.7 168.9 %copy-start = (f32[96,300]{1,0:T(8,128)S(1)}, f32[96,300]{1,0:T(8,128)}, u32[]{:S(2)}) copy-start(f32[96,300]{1,0:T(8,128)} %param.10) | copy-start | bytes 345604
  158.7 168.9 %copy-start.2 = (f32[96,300]{1,0:T(8,128)S(1)}, f32[96,300]{1,0:T(8,128)}, u32[]{:S(2)}) copy-start(f32[96,300]{1,0:T(8,128)} %param.12) | copy-start | bytes 345604
  158.7 307.3 %copy-start.1 = (f32[96,300]{1,0:T(8,128)S(1)}, f32[96,300]{1,0:T(8,128)}, u32[]{:S(2)}) copy-start(f32[96,300]{1,0:T(8,128)} %param.14) | copy-start | bytes 345604
  158.7 307.3 %copy-start.3 = (f32[96,300]{1,0:T(8,128)S(1)}, f32[96,300]{1,0:T(8,128)}, u32[]{:S(2)}) copy-start(f32[96,300]{1,0:T(8,128)} %param.16) | copy-start | bytes 345604
  158.7 307.3 %all-reduce.7.cloned.1.call-start = ((), (), s32[]{:S(2)}) async-start(), calls=%async_computation.2 | async-start | bytes 4718592 | tf_op jit(solution)/shard_map/psum | solution.py:67
Sparse Core Ops, SparseCore 0:
  158.8 168.7 all-reduce.4
  330.3 135.7 all-reduce.6
